TPU v7x, 512 devices: a whole 4x8x8 slice. The times are simulated.
512 devices in a mesh: blk: 16 (over z_lo, x), lab: 32 (over y, z_hi, core).
Axes of the slice: x: 4, y: 8, z: 8 (z_hi: 2, z_lo: 4; z = z_hi * 4 + z_lo), core: 2. Of those that a mesh axis runs over, the one named last changes fastest.
Arguments:
- features: bfloat16 [65536, 768], P(('blk', 'lab')), may hold values from -0.21875 to 0.21875
- direction: bfloat16 [32, 256, 768], P('lab', 'blk'), may hold values from -6 to 6
- active: int32 [65536, 8192], P('blk', 'lab'), may hold values 0 or 1
- shortlist: int32 [512, 64], P('blk', 'lab'), may hold values 0 or 1
Outputs:
- hess_product: float32 [32, 256, 768], P('lab', 'blk')
- curvature: float32 [32, 256], P('lab', 'blk')
All inputs are finite; a program needn't handle non-finite values. No bound on the sum of `active` or of `shortlist` on one device may be relied on, other than what follows from the above.
Results may differ from a plain program's by a relative error of at most 0.00059.
Values may be sent and summed in bfloat16 or wider, within the bound.
No kernel may reach another device: no remote copies, remote signals or barrier semaphores. Data moves between devices by JAX's collectives and lax.ppermute only.
A program may use at most 64 MiB of HBM per device.

v0:
```python
import jax
import jax.numpy as jnp
from jax import lax
from jax.sharding import PartitionSpec as P

D = 768
TILE = 128


def active_weights(active, shortlist):
    row_tiles, label_tiles = shortlist.shape
    blocks = active.reshape(row_tiles, TILE, label_tiles, TILE) * shortlist[:, None, :, None]
    return blocks.reshape(active.shape).astype(jnp.bfloat16)


def shards(features, direction, active, shortlist):
    vectors = direction[0]
    gathered = lax.all_gather(vectors, "blk", axis=0, tiled=True)
    weights = active_weights(active, shortlist)
    slab_part = lax.all_gather(features, "lab", axis=0, tiled=True)
    margins = lax.dot_general(
        slab_part, gathered, (((1,), (1,)), ((), ())), preferred_element_type=jnp.float32
    )
    scaled = (weights.astype(jnp.float32) * margins).astype(jnp.bfloat16)
    label_sums = lax.dot_general(
        scaled, slab_part, (((0,), (0,)), ((), ())), preferred_element_type=jnp.float32
    )
    own_total = lax.psum_scatter(label_sums, "blk", scatter_dimension=0, tiled=True)
    product = vectors.astype(jnp.float32) + own_total
    curve = jnp.sum(vectors.astype(jnp.float32) * product, axis=-1) / D
    return (product[None], curve[None])


def solution(mesh):
    return jax.shard_map(
        shards,
        mesh=mesh,
        in_specs=(P(("blk", "lab"), None), P("lab", "blk", None), P("blk", "lab"), P("blk", "lab")),
        out_specs=(P("lab", "blk", None), P("lab", "blk")),
        check_vma=False,
    )
```

profile of v0, /device:TPU:8, one launch (start us, length us, event | category | flops | bytes accessed | tf_op | source)
XLA Modules:
  0.0 245.1 jit_solution(11948266229189764883)
XLA Ops:
  7.2 0.0 all-gather.3.cloned.1.call-start
  7.2 0.7 all-gather.3.cloned.1.call-update
  7.9 0.0 reduce-scatter.2.cloned.1.call-start
  7.9 0.8 copy.6
  8.7 47.3 %all-gather = bf16[1,256,768]{2,1,0:T(8,128)(2,1)S(1)} all-gather(bf16[1,16,768]{2,1,0:T(8,128)(2,1)} %param.5), channel_id=2, replica_groups=mesh['blk'=16,'lab'=32] {'blk'}, dimensions={1}, use_global_device_ids=true | all-gather | bytes 417792 | tf_op jit(solution)/shard_map/all_gather | solution.py:18
  56.0 79.5 %all-gather.3.cloned.1.call-done = bf16[4096,768]{1,0:T(8,128)(2,1)} async-done(((bf16[128,768]{1,0:T(8,128)(2,1)}), bf16[4096,768]{1,0:T(8,128)(2,1)}) %all-gather.3.cloned.1.call-update) | async-done | bytes 6291472 | tf_op jit(solution)/shard_map/all_gather | solution.py:20
  135.5 3.2 %mul.17 = s32[32,128,2,128]{3,2,1,0:T(2,128)} broadcast(s32[32,2]{1,0:T(8,128)S(1)} %copy.6), dimensions={0,2} | broadcast | bytes 4194560 | tf_op jit(solution)/shard_map/mul | solution.py:12
  138.7 0.0 copy-start
  138.7 13.8 %fusion.4 = f32[256,768]{1,0:T(8,128)} fusion(bf16[4096,768]{1,0:T(8,128)(2,1)} %all-gather.3.cloned.1.call-done, s32[4096,256]{1,0:T(8,128)} %param.6, s32[512,8,2,128]{3,2,1,0:T(2,128)} %bitcast.25, bf16[1,256,768]{2,1,0:T(8,128)(2,1)S(1)} %all-gather), kind=kOutput, calls=%fused_computation.5 | convolution fusion | flops 3226468352 | bytes 15859712 | tf_op jit(solution)/shard_map/dot_general | solution.py:25
  152.5 0.0 reduce-scatter.2.cloned.1.call-update
  152.5 83.7 %reduce-scatter.2.cloned.1.call-done = f32[16,768]{1,0:T(8,128)} async-done(((f32[256,768]{1,0:T(8,128)}), f32[16,768]{1,0:T(8,128)}) %reduce-scatter.2.cloned.1.call-update) | async-done | bytes 49168 | tf_op jit(solution)/shard_map/reduce_scatter | solution.py:28
  236.2 0.0 copy-done
  236.2 1.5 fusion.6
  237.7 0.5 multiply_bitcast_fusion
Async XLA Ops:
  7.2 128.4 %all-gather.3.cloned.1.call-start = ((), (), s32[]{:S(2)}) async-start(), calls=%async_computation.1 | async-start | bytes 6488064 | tf_op jit(solution)/shard_map/all_gather | solution.py:20
  7.9 228.3 %reduce-scatter.2.cloned.1.call-start = ((), (), s32[]{:S(2)}) async-start(), calls=%async_computation.2 | async-start | bytes 835584 | tf_op jit(solution)/shard_map/reduce_scatter | solution.py:28
  138.7 97.5 %copy-start = (bf16[1,16,768]{2,1,0:T(8,128)(2,1)S(1)}, bf16[1,16,768]{2,1,0:T(8,128)(2,1)}, u32[]{:S(2)}) copy-start(bf16[1,16,768]{2,1,0:T(8,128)(2,1)} %param.5) | copy-start | bytes 73732
Sparse Core Ops, SparseCore 0:
  11.3 124.2 all-gather.2
  152.6 83.4 reduce-scatter.1
where the time goes:
time: 245 us
  waiting for transfers between devices  164 us (67%)
  blocking collectives  47.3 us (19%)
  between operations  14 us (6%)
  matrix products  13.8 us (6%)
  local copies, waits for them, and re-layouts  3.93 us (2%)
    reduce_scatter x1, waiting for transfers between devices, shards(): lax.psum_scatter(label_sums, 'blk', scatter_dimension=0, tiled=True)  83.7 us
    all_gather x1, waiting for transfers between devices, shards(): slab_part = lax.all_gather(features, 'lab', axis=0, tiled=True)  79.5 us
    all_gather x1, blocking collectives, shards(): gathered = lax.all_gather(vectors, 'blk', axis=0, tiled=True)  47.3 us
    dot_general x1, matrix products, shards(): lax.dot_general(scaled, slab_part, (((0,), (0,)), ((), ())), preferred_el...  13.8 us
  transfers between devices with their start and end apart: 2, of which 2 were waited for; matrix products, arithmetic and copies ran while one was open for 0% of the time, Pallas kernels for 0%

commit v1 on v0

v1 whole, which is shorter than its diff:
```python
import jax
import jax.numpy as jnp
from jax import lax
from jax.experimental import pallas as pl
from jax.experimental.pallas import tpu as pltpu
from jax.sharding import PartitionSpec as P


D = 768
TILE = 128
N_Y, N_H, N_CORE = 8, 2, 2
ROW_SCALE = 2.0 ** 17
SUM_SCALE = 4.0


def lab_index(y, h, c):
    return (y * N_H + h) * N_CORE + c


PLACES = [(y, h, c) for y in range(N_Y) for h in range(N_H) for c in range(N_CORE)]
ACROSS = [(lab_index(y, h, c), lab_index(y, 1 - h, c)) for y, h, c in PLACES]
CORE = [(lab_index(y, h, c), lab_index(y, h, 1 - c)) for y, h, c in PLACES]
RINGS = [[lab_index(y, h, c) for y in range(N_Y)] for h in range(N_H) for c in range(N_CORE)]


def weights_kernel(shortlist_ref, active_ref, out_ref):
    step = pl.program_id(0)
    tiles = active_ref.shape[0] // TILE
    for t in range(tiles):
        for j in range(active_ref.shape[1] // TILE):
            block = active_ref[t * TILE:(t + 1) * TILE, j * TILE:(j + 1) * TILE]
            block = block * shortlist_ref[j, step * tiles + t]
            block = block.astype(jnp.float32) * (1.0 / ROW_SCALE)
            out_ref[t, j * TILE:(j + 1) * TILE, :] = block.T.astype(jnp.bfloat16)


def make_weights(active, shortlist):
    rows, labels = active.shape
    per = 512
    return pl.pallas_call(
        weights_kernel,
        grid=(rows // per,),
        in_specs=[
            pl.BlockSpec(memory_space=pltpu.SMEM),
            pl.BlockSpec((per, labels), lambda i: (i, 0)),
        ],
        out_specs=pl.BlockSpec((per // TILE, labels, TILE), lambda i: (i, 0, 0)),
        out_shape=jax.ShapeDtypeStruct((rows // TILE, labels, TILE), jnp.bfloat16),
        compiler_params=pltpu.CompilerParams(vmem_limit_bytes=16 << 20),
        name="make_weights",
    )(shortlist, active)


def product_kernel(first, core_ref, d_ref, w_ref, rows_ref, *refs):
    out_ref = refs[-1]
    pair = N_H * TILE
    for y in range(N_Y):
        rows = rows_ref[y * pair:(y + 1) * pair, :]
        margins = lax.dot_general(
            d_ref[...], rows, (((1,), (1,)), ((), ())), preferred_element_type=jnp.float32
        )
        weights = jnp.concatenate([w_ref[lab_index(y, h, core_ref[0])] for h in range(N_H)], axis=1)
        scaled = (weights.astype(jnp.float32) * margins).astype(jnp.bfloat16)
        part = jnp.dot(scaled, rows, preferred_element_type=jnp.float32)
        if y:
            out_ref[...] += part
        elif first:
            out_ref[...] = part
        else:
            out_ref[...] = refs[0][...] + part


def label_sums(core, gathered, weights, slab, before):
    vmem = pl.BlockSpec(memory_space=pltpu.VMEM)
    first = before is None
    operands = [core, gathered, weights, slab, *([] if first else [before])]

    def body(*refs):
        product_kernel(first, *refs)

    return pl.pallas_call(
        body,
        in_specs=[pl.BlockSpec(memory_space=pltpu.SMEM), *[vmem] * (len(operands) - 1)],
        out_specs=vmem,
        out_shape=jax.ShapeDtypeStruct(gathered.shape, jnp.float32),
        input_output_aliases={} if first else {4: 0},
        cost_estimate=pl.CostEstimate(
            flops=4 * slab.size * gathered.shape[0], bytes_accessed=2 * slab.size, transcendentals=0
        ),
        compiler_params=pltpu.CompilerParams(vmem_limit_bytes=8 << 20),
        name="label_sums",
    )(*operands)


def repeat_kernel(in_ref, out_ref):
    for place in range(out_ref.shape[0]):
        out_ref[place] = in_ref[...]


def repeat(vectors, times):
    vmem = pl.BlockSpec(memory_space=pltpu.VMEM)
    return pl.pallas_call(
        repeat_kernel,
        in_specs=[vmem],
        out_specs=vmem,
        out_shape=jax.ShapeDtypeStruct((times, *vectors.shape), vectors.dtype),
        compiler_params=pltpu.CompilerParams(vmem_limit_bytes=4 << 20),
        name="repeat",
    )(vectors)


def label_scale(vectors):
    return jnp.maximum(jnp.max(jnp.abs(vectors.astype(jnp.float32)), axis=-1, keepdims=True), 1e-30)


def shards(features, direction, active, shortlist):
    return steps(features, direction[0], active, shortlist)


def steps(features, vectors, active, shortlist):
    lab = lax.axis_index("lab")
    h, core = (lab & N_CORE) // N_CORE, (lab & 1).astype(jnp.int32).reshape(1)
    across = lax.ppermute(features, "lab", ACROSS)
    gathered = lax.all_to_all(repeat(vectors, 16), "blk", 0, 0, tiled=True).reshape(-1, D)
    pair = jnp.where(h == 0, jnp.stack([features, across]), jnp.stack([across, features]))
    pair = (pair.astype(jnp.float32) * ROW_SCALE).astype(jnp.float16).reshape(-1, D)
    slab = lax.all_gather(pair, "lab", axis_index_groups=RINGS, axis=0, tiled=True)
    beside = lax.ppermute(slab, "lab", CORE)
    slab, active = lax.optimization_barrier((slab, active))
    weights = make_weights(active, shortlist.T)
    sums = label_sums(core, gathered, weights, slab.astype(jnp.bfloat16), None)
    sums = label_sums(1 - core, gathered, weights, beside.astype(jnp.bfloat16), sums)
    sent = (sums * (1.0 / (SUM_SCALE * ROW_SCALE * label_scale(gathered)))).astype(jnp.float16)
    sent, own_scale = lax.optimization_barrier((sent, SUM_SCALE * label_scale(vectors)))
    pieces = lax.all_to_all(sent.reshape(16, 16, D), "blk", 0, 0, tiled=True)
    own_total = jnp.sum(pieces.astype(jnp.float32), axis=0) * own_scale
    product = vectors.astype(jnp.float32) + own_total
    curve = jnp.sum(vectors.astype(jnp.float32) * product, axis=-1) / D
    return (product[None], curve[None])


def solution(mesh):
    return jax.shard_map(
        shards,
        mesh=mesh,
        in_specs=(P(("blk", "lab"), None), P("lab", "blk", None), P("blk", "lab"), P("blk", "lab")),
        out_specs=(P("lab", "blk", None), P("lab", "blk")),
        check_vma=False,
    )
```

time: 245 us -> 109 us (0.44)
  the two profiles are of different devices: /device:TPU:8 before, /device:TPU:24 now
where the time goes in v1:
time: 109 us
  blocking collectives  53.1 us (49%)
  starting transfers between devices  23.4 us (21%)
  waiting for transfers between devices  12.6 us (12%)
  other arithmetic  9.65 us (9%)
  Pallas kernels  7.07 us (6%)
  local copies, waits for them, and re-layouts  1.99 us (2%)
    all_gather x1, blocking collectives, steps(): lax.all_gather(pair, 'lab', axis_index_groups=RINGS, axis=0, tiled=True)  36.7 us
    all_to_all x1, blocking collectives, steps(): pieces = lax.all_to_all(sent.reshape(16, 16, D), 'blk', 0, 0, tiled=True)  16.5 us
    ppermute x1, starting transfers between devices, steps(): across = lax.ppermute(features, 'lab', ACROSS)  10.9 us
    all_to_all x1, starting transfers between devices, steps(): lax.all_to_all(repeat(vectors, 16), 'blk', 0, 0, tiled=True).reshape(-1, D)  10.5 us
    all_to_all x1, waiting for transfers between devices, steps(): lax.all_to_all(repeat(vectors, 16), 'blk', 0, 0, tiled=True).reshape(-1, D)  7.45 us
    ppermute x1, waiting for transfers between devices, steps(): across = lax.ppermute(features, 'lab', ACROSS)  5.18 us
    pallas_call x2, Pallas kernels, label_sums(): pl.pallas_call(body, in_specs=[pl.BlockSpec(memory_space=pltpu.SMEM), *[v...  4.47 us
    convert_element_type x1, other arithmetic, steps(): sums = label_sums(core, gathered, weights, slab.astype(jnp.bfloat16), None)  4.22 us
  transfers between devices with their start and end apart: 3, of which 2 were waited for; matrix products, arithmetic and copies ran while one was open for 4% of the time, Pallas kernels for 4%

profile of v1, /device:TPU:24, one launch (start us, length us, event | category | flops | bytes accessed | tf_op | source)
XLA Modules:
  0.0 108.6 jit_solution(2660163434652775293)
XLA Ops:
  0.6 0.0 copy-start.2
  0.6 10.9 %collective-permute-start = (bf16[128,768]{1,0:T(8,128)(2,1)}, bf16[128,768]{1,0:T(8,128)(2,1)S(1)}, u32[]{:S(2)}, u32[]{:S(2)}) collective-permute-start(bf16[128,768]{1,0:T(8,128)(2,1)} %param.4), channel_id=1, source_target_pairs={{0,2},{1,3},{2,0},{3,1},{4,6},{5,7},{6,4},{7,5},{8,10},{9,11},{10,... | collective-permute-start | bytes 589832 | tf_op jit(solution)/shard_map/ppermute | solution.py:123
  11.6 5.2 %collective-permute-done = bf16[128,768]{1,0:T(8,128)(2,1)S(1)} collective-permute-done((bf16[128,768]{1,0:T(8,128)(2,1)}, bf16[128,768]{1,0:T(8,128)(2,1)S(1)}, u32[]{:S(2)}, u32[]{:S(2)}) %collective-permute-start) | collective-permute-done | bytes 196640 | tf_op jit(solution)/shard_map/ppermute | solution.py:123
  16.8 1.2 %multiply_convert_fusion.1 = f16[2,128,768]{2,1,0:T(8,128)(2,1)S(1)} fusion(bf16[1,128,768]{2,1,0:T(8,128)(2,1)S(1)} %bitcast.26, bf16[1,128,768]{2,1,0:T(8,128)(2,1)} %bitcast.25, pred[]{:T(512)S(6)} %eq.3), kind=kLoop, calls=%fused_computation.3 | loop fusion | flops 1179648 | bytes 786433 | tf_op jit(solution)/shard_map/convert_element_type | solution.py:126
  18.0 36.7 %all-gather.1 = f16[2048,768]{1,0:T(8,128)(2,1)} all-gather(f16[256,768]{1,0:T(8,128)(2,1)S(1)} %bitcast.23), channel_id=1, replica_groups={{0,4,8,12,16,20,24,28},{1,5,9,13,17,21,25,29},{2,6,10,14,18,22,26,30},{..., dimensions={0}, use_global_device_ids=true | all-gather | bytes 3538944 | tf_op jit(solution)/shard_map/all_gather | solution.py:127
  54.6 1.9 %collective-permute-start.1 = (f16[2048,768]{1,0:T(8,128)(2,1)}, f16[2048,768]{1,0:T(8,128)(2,1)}, u32[]{:S(2)}, u32[]{:S(2)}) collective-permute-start(f16[2048,768]{1,0:T(8,128)(2,1)} %all-gather.1), channel_id=1, source_target_pairs={{0,1},{1,0},{2,3},{3,2},{4,5},{5,4},{6,7},{7,6},{8,9},{9,8},{10,11... | collective-permute-start | bytes 9437192 | tf_op jit(solution)/shard_map/ppermute | solution.py:128
  56.5 0.0 copy-done.2
  56.6 0.8 repeat.1
  57.3 10.5 %all-to-all-start = ((bf16[16,16,768]{2,1,0:T(8,128)(2,1)}), bf16[16,16,768]{2,1,0:T(8,128)(2,1)S(1)}, u32[]{:S(2)}, u32[]{:S(2)}) async-start(bf16[16,16,768]{2,1,0:T(8,128)(2,1)} %repeat.1), calls=%async_computation | async-start | bytes 786432 | tf_op jit(solution)/shard_map/all_to_all | solution.py:124
  67.9 0.1 fusion
  68.0 0.0 copy-start.1
  68.0 0.0 copy-start.3
  68.0 4.2 %convert_element_type.41.refs_3_ = bf16[2048,768]{1,0:T(8,128)(2,1)} convert(f16[2048,768]{1,0:T(8,128)(2,1)} %all-gather.1) | non-fusion elementwise | flops 1572864 | bytes 6291456 | tf_op jit(solution)/shard_map/convert_element_type | solution.py:131
  72.2 0.0 copy-done.1
  72.2 0.0 copy-done.3
  72.2 1.8 %make_weights.1.refs_2_ = bf16[32,256,128]{2,1,0:T(8,128)(2,1)S(1)} custom-call(s32[2,32]{1,0:T(2,128)S(1)} %bitcast.22, s32[4096,256]{1,0:T(8,128)S(1)} %copy-done.1), custom_call_target="tpu_custom_call" | custom-call | tf_op jit(solution)/shard_map/make_weights/pallas_call | solution.py:40
  74.1 7.4 %all-to-all-done = bf16[16,16,768]{2,1,0:T(8,128)(2,1)S(1)} async-done(((bf16[16,16,768]{2,1,0:T(8,128)(2,1)}), bf16[16,16,768]{2,1,0:T(8,128)(2,1)S(1)}, u32[]{:S(2)}, u32[]{:S(2)}) %all-to-all-start) | async-done | bytes 393248 | tf_op jit(solution)/shard_map/all_to_all | solution.py:124
  81.5 0.1 abs_reduce_fusion
  81.7 0.1 div.32
  81.8 0.0 copy-start
  81.8 1.9 %copy-done = bf16[2048,768]{1,0:T(8,128)(2,1)S(1)} copy-done((bf16[2048,768]{1,0:T(8,128)(2,1)S(1)}, bf16[2048,768]{1,0:T(8,128)(2,1)}, u32[]{:S(2)}) %copy-start) | copy-done | bytes 3145752
  83.7 2.2 %label_sums.2.refs_4_ = f32[256,768]{1,0:T(8,128)S(1)} custom-call(s32[1]{0:T(128)} %bitcast.refs_0_, bf16[256,768]{1,0:T(8,128)(2,1)S(1)} %bitcast.19, bf16[32,256,128]{2,1,0:T(8,128)(2,1)S(1)} %make_weights.1.refs_2_, bf16[2048,768]{1,0:T(8,128)(2,1)S(1)} %copy-done), custom_call_target="tpu_custom_call" | custom-call | flops 1610612736 | bytes 3145728 | tf_op jit(solution)/shard_map/label_sums/pallas_call | solution.py:81
  85.9 0.0 collective-permute-done.1
  85.9 2.4 %convert_element_type.40.refs_3_ = bf16[2048,768]{1,0:T(8,128)(2,1)S(1)} convert(f16[2048,768]{1,0:T(8,128)(2,1)} %collective-permute-done.1) | non-fusion elementwise | flops 1572864 | bytes 6291456 | tf_op jit(solution)/shard_map/convert_element_type | solution.py:132
  88.3 2.3 %label_sums.3 = f32[256,768]{1,0:T(8,128)S(1)} custom-call(s32[1]{0:T(128)S(6)} %sub.7.refs_0_, bf16[256,768]{1,0:T(8,128)(2,1)S(1)} %bitcast.20, bf16[32,256,128]{2,1,0:T(8,128)(2,1)S(1)} %make_weights.1.refs_2_, bf16[2048,768]{1,0:T(8,128)(2,1)S(1)} %convert_element_type.40.refs_3_, f32[256,768]{1,0:T(8,128)S(1)} %label_sums.2.refs_4_), custom_call_target="tpu_custom_call", output_to_operand_aliasing={{}: (4, {})} | custom-call | flops 1610612736 | bytes 3145728 | tf_op jit(solution)/shard_map/label_sums/pallas_call | solution.py:81
  90.5 0.1 multiply_convert_fusion
  90.7 16.5 %all_to_all.10 = f16[16,16,768]{2,1,0:T(8,128)(2,1)S(1)} all-to-all(f16[16,16,768]{2,1,0:T(8,128)(2,1)S(1)} %bitcast.24), channel_id=1, replica_groups=mesh['blk'=16,'lab'=32] {'blk'}, dimensions={0} | all-to-all | bytes 786432 | tf_op jit(solution)/shard_map/all_to_all | solution.py:135
  107.2 0.1 convert_reduce_fusion
  107.2 0.2 fusion.1
  107.4 0.7 fusion.2
  108.1 0.5 multiply_bitcast_fusion
  (2 shorter events, 0.0 us)
Async XLA Ops:
  0.6 55.9 %copy-start.2 = (bf16[1,16,768]{2,1,0:T(8,128)(2,1)S(1)}, bf16[1,16,768]{2,1,0:T(8,128)(2,1)}, u32[]{:S(2)}) copy-start(bf16[1,16,768]{2,1,0:T(8,128)(2,1)} %param.5) | copy-start | bytes 73732
  0.6 16.1 %collective-permute-start = (bf16[128,768]{1,0:T(8,128)(2,1)}, bf16[128,768]{1,0:T(8,128)(2,1)S(1)}, u32[]{:S(2)}, u32[]{:S(2)}) collective-permute-start(bf16[128,768]{1,0:T(8,128)(2,1)} %param.4), channel_id=1, source_target_pairs={{0,2},{1,3},{2,0},{3,1},{4,6},{5,7},{6,4},{7,5},{8,10},{9,11},{10,... | collective-permute-start | bytes 589832 | tf_op jit(solution)/shard_map/ppermute | solution.py:123
  54.6 31.2 %collective-permute-start.1 = (f16[2048,768]{1,0:T(8,128)(2,1)}, f16[2048,768]{1,0:T(8,128)(2,1)}, u32[]{:S(2)}, u32[]{:S(2)}) collective-permute-start(f16[2048,768]{1,0:T(8,128)(2,1)} %all-gather.1), channel_id=1, source_target_pairs={{0,1},{1,0},{2,3},{3,2},{4,5},{5,4},{6,7},{7,6},{8,9},{9,8},{10,11... | collective-permute-start | bytes 9437192 | tf_op jit(solution)/shard_map/ppermute | solution.py:128
  57.3 24.2 %all-to-all-start = ((bf16[16,16,768]{2,1,0:T(8,128)(2,1)}), bf16[16,16,768]{2,1,0:T(8,128)(2,1)S(1)}, u32[]{:S(2)}, u32[]{:S(2)}) async-start(bf16[16,16,768]{2,1,0:T(8,128)(2,1)} %repeat.1), calls=%async_computation | async-start | bytes 786432 | tf_op jit(solution)/shard_map/all_to_all | solution.py:124
  68.0 4.2 %copy-start.1 = (s32[4096,256]{1,0:T(8,128)S(1)}, s32[4096,256]{1,0:T(8,128)}, u32[]{:S(2)}) copy-start(s32[4096,256]{1,0:T(8,128)} %active_ref) | copy-start | bytes 12582916
  68.0 4.2 %copy-start.3 = (s32[32,2]{0,1:T(2,128)S(1)}, s32[32,2]{0,1:T(2,128)}, u32[]{:S(2)}) copy-start(s32[32,2]{0,1:T(2,128)} %param.7) | copy-start | bytes 772
  81.8 1.9 %copy-start = (bf16[2048,768]{1,0:T(8,128)(2,1)S(1)}, bf16[2048,768]{1,0:T(8,128)(2,1)}, u32[]{:S(2)}) copy-start(bf16[2048,768]{1,0:T(8,128)(2,1)} %convert_element_type.41.refs_3_) | copy-start | bytes 9437188

commit v2 on v1

--- a/solution.py
+++ b/solution.py
@@ -11,6 +11,9 @@
 N_Y, N_H, N_CORE = 8, 2, 2
 ROW_SCALE = 2.0 ** 17
 SUM_SCALE = 4.0
+VMEM_LIMIT = 48 << 20
+N_PARTS = 4
+STOPS = (0, 2, 5, 8)
 
 
 def lab_index(y, h, c):
@@ -23,38 +26,51 @@
 RINGS = [[lab_index(y, h, c) for y in range(N_Y)] for h in range(N_H) for c in range(N_CORE)]
 
 
-def weights_kernel(shortlist_ref, active_ref, out_ref):
-    step = pl.program_id(0)
-    tiles = active_ref.shape[0] // TILE
+def weights_kernel(shortlist_ref, active_hbm, out_ref, active_ref, arrived):
+    tiles, labels = active_ref.shape[0] // TILE, active_ref.shape[1]
+    per = tiles // N_PARTS
+
+    def fetch(part):
+        rows = pl.ds(part * per * TILE, per * TILE)
+        return pltpu.make_async_copy(active_hbm.at[rows, :], active_ref.at[rows, :], arrived.at[part])
+
+    for part in range(N_PARTS):
+        fetch(part).start()
     for t in range(tiles):
-        for j in range(active_ref.shape[1] // TILE):
+        if t % per == 0:
+            fetch(t // per).wait()
+        for j in range(labels // TILE):
             block = active_ref[t * TILE:(t + 1) * TILE, j * TILE:(j + 1) * TILE]
-            block = block * shortlist_ref[j, step * tiles + t]
-            block = block.astype(jnp.float32) * (1.0 / ROW_SCALE)
+            block = (block * shortlist_ref[j, t]).astype(jnp.float32) * (1.0 / ROW_SCALE)
             out_ref[t, j * TILE:(j + 1) * TILE, :] = block.T.astype(jnp.bfloat16)
 
 
 def make_weights(active, shortlist):
     rows, labels = active.shape
-    per = 512
     return pl.pallas_call(
         weights_kernel,
-        grid=(rows // per,),
-        in_specs=[
-            pl.BlockSpec(memory_space=pltpu.SMEM),
-            pl.BlockSpec((per, labels), lambda i: (i, 0)),
-        ],
-        out_specs=pl.BlockSpec((per // TILE, labels, TILE), lambda i: (i, 0, 0)),
+        in_specs=[pl.BlockSpec(memory_space=pltpu.SMEM), pl.BlockSpec(memory_space=pl.ANY)],
+        out_specs=pl.BlockSpec(memory_space=pltpu.VMEM),
         out_shape=jax.ShapeDtypeStruct((rows // TILE, labels, TILE), jnp.bfloat16),
-        compiler_params=pltpu.CompilerParams(vmem_limit_bytes=16 << 20),
+        scratch_shapes=[pltpu.VMEM(active.shape, jnp.int32), pltpu.SemaphoreType.DMA((N_PARTS,))],
+        compiler_params=pltpu.CompilerParams(vmem_limit_bytes=VMEM_LIMIT),
         name="make_weights",
     )(shortlist, active)
 
 
-def product_kernel(first, core_ref, d_ref, w_ref, rows_ref, *refs):
-    out_ref = refs[-1]
+def product_kernel(first, core_ref, d_ref, w_ref, rows_hbm, *refs):
+    before, (out_ref, rows_ref, arrived) = refs[:-3], refs[-3:]
     pair = N_H * TILE
+
+    def fetch(part):
+        rows = pl.ds(STOPS[part] * pair, (STOPS[part + 1] - STOPS[part]) * pair)
+        return pltpu.make_async_copy(rows_hbm.at[rows, :], rows_ref.at[rows, :], arrived.at[part])
+
+    for part in range(len(STOPS) - 1):
+        fetch(part).start()
     for y in range(N_Y):
+        if y in STOPS:
+            fetch(STOPS.index(y)).wait()
         rows = rows_ref[y * pair:(y + 1) * pair, :]
         margins = lax.dot_general(
             d_ref[...], rows, (((1,), (1,)), ((), ())), preferred_element_type=jnp.float32
@@ -67,7 +83,7 @@
         elif first:
             out_ref[...] = part
         else:
-            out_ref[...] = refs[0][...] + part
+            out_ref[...] = before[0][...] + part
 
 
 def label_sums(core, gathered, weights, slab, before):
@@ -80,14 +96,20 @@
 
     return pl.pallas_call(
         body,
-        in_specs=[pl.BlockSpec(memory_space=pltpu.SMEM), *[vmem] * (len(operands) - 1)],
+        in_specs=[
+            pl.BlockSpec(memory_space=pltpu.SMEM), vmem, vmem, pl.BlockSpec(memory_space=pl.ANY),
+            *([] if first else [vmem]),
+        ],
         out_specs=vmem,
         out_shape=jax.ShapeDtypeStruct(gathered.shape, jnp.float32),
+        scratch_shapes=[
+            pltpu.VMEM(slab.shape, jnp.bfloat16), pltpu.SemaphoreType.DMA((len(STOPS) - 1,)),
+        ],
         input_output_aliases={} if first else {4: 0},
         cost_estimate=pl.CostEstimate(
             flops=4 * slab.size * gathered.shape[0], bytes_accessed=2 * slab.size, transcendentals=0
         ),
-        compiler_params=pltpu.CompilerParams(vmem_limit_bytes=8 << 20),
+        compiler_params=pltpu.CompilerParams(vmem_limit_bytes=VMEM_LIMIT),
         name="label_sums",
     )(*operands)
 
@@ -125,11 +147,11 @@
     pair = jnp.where(h == 0, jnp.stack([features, across]), jnp.stack([across, features]))
     pair = (pair.astype(jnp.float32) * ROW_SCALE).astype(jnp.float16).reshape(-1, D)
     slab = lax.all_gather(pair, "lab", axis_index_groups=RINGS, axis=0, tiled=True)
+    slab = slab.astype(jnp.bfloat16)
     beside = lax.ppermute(slab, "lab", CORE)
-    slab, active = lax.optimization_barrier((slab, active))
     weights = make_weights(active, shortlist.T)
-    sums = label_sums(core, gathered, weights, slab.astype(jnp.bfloat16), None)
-    sums = label_sums(1 - core, gathered, weights, beside.astype(jnp.bfloat16), sums)
+    sums = label_sums(core, gathered, weights, slab, None)
+    sums = label_sums(1 - core, gathered, weights, beside, sums)
     sent = (sums * (1.0 / (SUM_SCALE * ROW_SCALE * label_scale(gathered)))).astype(jnp.float16)
     sent, own_scale = lax.optimization_barrier((sent, SUM_SCALE * label_scale(vectors)))
     pieces = lax.all_to_all(sent.reshape(16, 16, D), "blk", 0, 0, tiled=True)

time: 109 us -> 109 us (level)
  Pallas kernels: 7.07 us -> 11.8 us
  other arithmetic: 9.65 us -> 5.17 us
  waiting for transfers between devices: 12.6 us -> 15.7 us
  local copies, waits for them, and re-layouts: 1.99 us -> 0.09 us
  blocking collectives: 53.1 us -> 52 us
    pallas_call x3, Pallas kernels: 6.3 us -> 11 us  [the longest x2 7.98 us: label_sums(): pl.pallas_call(body, in_specs=[pl.BlockSpec(memory_space=pltpu.SMEM), vme...]
    convert_element_type x2 -> x1, other arithmetic: 6.59 us -> 2.15 us  [steps(): slab = slab.astype(jnp.bfloat16)]
    all_to_all x1, waiting for transfers between devices: 7.45 us -> 10.5 us  [steps(): lax.all_to_all(repeat(vectors, 16), 'blk', 0, 0, tiled=True).reshape(-1, D)]
    unnamed x8 -> x4, local copies, waits for them, and re-layouts: 1.91 us -> 0.01 us
    all_gather x1, blocking collectives: 36.7 us -> 35.5 us  [steps(): lax.all_gather(pair, 'lab', axis_index_groups=RINGS, axis=0, tiled=True)]
  transfers between devices with their start and end apart: 3 -> 3, of which waited for: 2 -> 2; matrix products, arithmetic and copies ran while one was open for 4% -> 0% of each run, Pallas kernels for 4% -> 7%
where the time goes in v2:
time: 109 us
  blocking collectives  52 us (48%)
  starting transfers between devices  23.2 us (21%)
  waiting for transfers between devices  15.7 us (14%)
  Pallas kernels  11.8 us (11%)
  other arithmetic  5.17 us (5%)
    all_gather x1, blocking collectives, steps(): lax.all_gather(pair, 'lab', axis_index_groups=RINGS, axis=0, tiled=True)  35.5 us
    all_to_all x1, blocking collectives, steps(): pieces = lax.all_to_all(sent.reshape(16, 16, D), 'blk', 0, 0, tiled=True)  16.5 us
    ppermute x1, starting transfers between devices, steps(): across = lax.ppermute(features, 'lab', ACROSS)  10.9 us
    all_to_all x1, waiting for transfers between devices, steps(): lax.all_to_all(repeat(vectors, 16), 'blk', 0, 0, tiled=True).reshape(-1, D)  10.5 us
    all_to_all x1, starting transfers between devices, steps(): lax.all_to_all(repeat(vectors, 16), 'blk', 0, 0, tiled=True).reshape(-1, D)  10.4 us
    pallas_call x2, Pallas kernels, label_sums(): pl.pallas_call(body, in_specs=[pl.BlockSpec(memory_space=pltpu.SMEM), vme...  7.98 us
    ppermute x1, waiting for transfers between devices, steps(): across = lax.ppermute(features, 'lab', ACROSS)  5.18 us
    pallas_call x1, Pallas kernels, make_weights(): pl.pallas_call(weights_kernel, in_specs=[pl.BlockSpec(memory_space=pltpu....  2.98 us
  transfers between devices with their start and end apart: 3, of which 2 were waited for; matrix products, arithmetic and copies ran while one was open for 0% of the time, Pallas kernels for 7%

profile of v2, /device:TPU:24, one launch (start us, length us, event | category | flops | bytes accessed | tf_op | source)
XLA Modules:
  0.0 108.7 jit_solution(16976251652036102361)
XLA Ops:
  0.6 10.9 %collective-permute-start = (bf16[128,768]{1,0:T(8,128)(2,1)}, bf16[128,768]{1,0:T(8,128)(2,1)S(1)}, u32[]{:S(2)}, u32[]{:S(2)}) collective-permute-start(bf16[128,768]{1,0:T(8,128)(2,1)} %param.4), channel_id=1, source_target_pairs={{0,2},{1,3},{2,0},{3,1},{4,6},{5,7},{6,4},{7,5},{8,10},{9,11},{10,... | collective-permute-start | bytes 589832 | tf_op jit(solution)/shard_map/ppermute | solution.py:145
  11.6 5.2 %collective-permute-done = bf16[128,768]{1,0:T(8,128)(2,1)S(1)} collective-permute-done((bf16[128,768]{1,0:T(8,128)(2,1)}, bf16[128,768]{1,0:T(8,128)(2,1)S(1)}, u32[]{:S(2)}, u32[]{:S(2)}) %collective-permute-start) | collective-permute-done | bytes 196640 | tf_op jit(solution)/shard_map/ppermute | solution.py:145
  16.7 1.2 %multiply_convert_fusion.1 = f16[2,128,768]{2,1,0:T(8,128)(2,1)S(1)} fusion(bf16[1,128,768]{2,1,0:T(8,128)(2,1)S(1)} %bitcast.26, bf16[1,128,768]{2,1,0:T(8,128)(2,1)} %bitcast.25, pred[]{:T(512)S(6)} %eq.3), kind=kLoop, calls=%fused_computation.3 | loop fusion | flops 1179648 | bytes 786433 | tf_op jit(solution)/shard_map/convert_element_type | solution.py:148
  17.9 35.5 %all-gather.1 = f16[2048,768]{1,0:T(8,128)(2,1)S(1)} all-gather(f16[256,768]{1,0:T(8,128)(2,1)S(1)} %bitcast.23), channel_id=1, replica_groups={{0,4,8,12,16,20,24,28},{1,5,9,13,17,21,25,29},{2,6,10,14,18,22,26,30},{..., dimensions={0}, use_global_device_ids=true | all-gather | bytes 3538944 | tf_op jit(solution)/shard_map/all_gather | solution.py:149
  53.5 0.0 copy-start
  53.5 0.0 copy-start.1
  53.5 2.1 %convert_element_type.37.refs_3_ = bf16[2048,768]{1,0:T(8,128)(2,1)} convert(f16[2048,768]{1,0:T(8,128)(2,1)S(1)} %all-gather.1) | non-fusion elementwise | flops 1572864 | bytes 6291456 | tf_op jit(solution)/shard_map/convert_element_type | solution.py:150
  55.6 1.9 %collective-permute-start.1 = (bf16[2048,768]{1,0:T(8,128)(2,1)}, bf16[2048,768]{1,0:T(8,128)(2,1)}, u32[]{:S(2)}, u32[]{:S(2)}) collective-permute-start(bf16[2048,768]{1,0:T(8,128)(2,1)} %convert_element_type.37.refs_3_), channel_id=1, source_target_pairs={{0,1},{1,0},{2,3},{3,2},{4,5},{5,4},{6,7},{7,6},{8,9},{9,8},{10,11... | collective-permute-start | bytes 9437192 | tf_op jit(solution)/shard_map/ppermute | solution.py:151
  57.5 0.0 copy-done
  57.5 0.8 repeat.1
  58.3 10.4 %all-to-all-start = ((bf16[16,16,768]{2,1,0:T(8,128)(2,1)}), bf16[16,16,768]{2,1,0:T(8,128)(2,1)S(1)}, u32[]{:S(2)}, u32[]{:S(2)}) async-start(bf16[16,16,768]{2,1,0:T(8,128)(2,1)} %repeat.1), calls=%async_computation | async-start | bytes 786432 | tf_op jit(solution)/shard_map/all_to_all | solution.py:146
  68.8 0.0 copy-done.1
  68.8 3.0 %make_weights.1.refs_2_ = bf16[32,256,128]{2,1,0:T(8,128)(2,1)S(1)} custom-call(s32[2,32]{1,0:T(2,128)S(1)} %bitcast.22, s32[4096,256]{1,0:T(8,128)} %active_hbm.1), custom_call_target="tpu_custom_call" | custom-call | tf_op jit(solution)/shard_map/make_weights/pallas_call | solution.py:50
  71.8 0.1 fusion
  71.9 10.5 %all-to-all-done = bf16[16,16,768]{2,1,0:T(8,128)(2,1)S(1)} async-done(((bf16[16,16,768]{2,1,0:T(8,128)(2,1)}), bf16[16,16,768]{2,1,0:T(8,128)(2,1)S(1)}, u32[]{:S(2)}, u32[]{:S(2)}) %all-to-all-start) | async-done | bytes 393248 | tf_op jit(solution)/shard_map/all_to_all | solution.py:146
  82.4 0.1 abs_reduce_fusion
  82.6 0.1 div.32
  82.7 4.0 %label_sums.2.refs_4_ = f32[256,768]{1,0:T(8,128)S(1)} custom-call(s32[1]{0:T(128)} %bitcast.refs_0_, bf16[256,768]{1,0:T(8,128)(2,1)S(1)} %bitcast.19, bf16[32,256,128]{2,1,0:T(8,128)(2,1)S(1)} %make_weights.1.refs_2_, bf16[2048,768]{1,0:T(8,128)(2,1)} %convert_element_type.37.refs_3_), custom_call_target="tpu_custom_call" | custom-call | flops 1610612736 | bytes 3145728 | tf_op jit(solution)/shard_map/label_sums/pallas_call | solution.py:97
  86.7 0.0 collective-permute-done.1.refs_3_
  86.7 4.0 %label_sums.3 = f32[256,768]{1,0:T(8,128)S(1)} custom-call(s32[1]{0:T(128)S(6)} %sub.7.refs_0_, bf16[256,768]{1,0:T(8,128)(2,1)S(1)} %bitcast.20, bf16[32,256,128]{2,1,0:T(8,128)(2,1)S(1)} %make_weights.1.refs_2_, bf16[2048,768]{1,0:T(8,128)(2,1)} %collective-permute-done.1.refs_3_, f32[256,768]{1,0:T(8,128)S(1)} %label_sums.2.refs_4_), custom_call_target="tpu_custom_call", output_to_operand_aliasing={{}: (4, {})} | custom-call | flops 1610612736 | bytes 3145728 | tf_op jit(solution)/shard_map/label_sums/pallas_call | solution.py:97
  90.7 0.1 multiply_convert_fusion
  90.8 16.5 %all_to_all.10 = f16[16,16,768]{2,1,0:T(8,128)(2,1)S(1)} all-to-all(f16[16,16,768]{2,1,0:T(8,128)(2,1)S(1)} %bitcast.24), channel_id=1, replica_groups=mesh['blk'=16,'lab'=32] {'blk'}, dimensions={0} | all-to-all | bytes 786432 | tf_op jit(solution)/shard_map/all_to_all | solution.py:157
  107.3 0.1 convert_reduce_fusion
  107.3 0.7 fusion.2
  108.0 0.2 fusion.1
  108.2 0.5 multiply_bitcast_fusion
  (2 shorter events, 0.0 us)
Async XLA Ops:
  0.6 16.1 %collective-permute-start = (bf16[128,768]{1,0:T(8,128)(2,1)}, bf16[128,768]{1,0:T(8,128)(2,1)S(1)}, u32[]{:S(2)}, u32[]{:S(2)}) collective-permute-start(bf16[128,768]{1,0:T(8,128)(2,1)} %param.4), channel_id=1, source_target_pairs={{0,2},{1,3},{2,0},{3,1},{4,6},{5,7},{6,4},{7,5},{8,10},{9,11},{10,... | collective-permute-start | bytes 589832 | tf_op jit(solution)/shard_map/ppermute | solution.py:145
  53.5 4.1 %copy-start = (bf16[1,16,768]{2,1,0:T(8,128)(2,1)S(1)}, bf16[1,16,768]{2,1,0:T(8,128)(2,1)}, u32[]{:S(2)}) copy-start(bf16[1,16,768]{2,1,0:T(8,128)(2,1)} %param.5) | copy-start | bytes 73732
  53.5 15.3 %copy-start.1 = (s32[32,2]{0,1:T(2,128)S(1)}, s32[32,2]{0,1:T(2,128)}, u32[]{:S(2)}) copy-start(s32[32,2]{0,1:T(2,128)} %param.7) | copy-start | bytes 772
  55.6 31.1 %collective-permute-start.1 = (bf16[2048,768]{1,0:T(8,128)(2,1)}, bf16[2048,768]{1,0:T(8,128)(2,1)}, u32[]{:S(2)}, u32[]{:S(2)}) collective-permute-start(bf16[2048,768]{1,0:T(8,128)(2,1)} %convert_element_type.37.refs_3_), channel_id=1, source_target_pairs={{0,1},{1,0},{2,3},{3,2},{4,5},{5,4},{6,7},{7,6},{8,9},{9,8},{10,11... | collective-permute-start | bytes 9437192 | tf_op jit(solution)/shard_map/ppermute | solution.py:151
  58.3 24.1 %all-to-all-start = ((bf16[16,16,768]{2,1,0:T(8,128)(2,1)}), bf16[16,16,768]{2,1,0:T(8,128)(2,1)S(1)}, u32[]{:S(2)}, u32[]{:S(2)}) async-start(bf16[16,16,768]{2,1,0:T(8,128)(2,1)} %repeat.1), calls=%async_computation | async-start | bytes 786432 | tf_op jit(solution)/shard_map/all_to_all | solution.py:146

commit v3 on v2

v3 whole, which is shorter than its diff:
```python
import jax
import jax.numpy as jnp
from jax import lax
from jax.experimental import pallas as pl
from jax.experimental.pallas import tpu as pltpu
from jax.sharding import PartitionSpec as P


D = 768
TILE = 128
N_Y, N_H, N_CORE = 8, 2, 2
ROW_SCALE = 2.0 ** 17
SUM_SCALE = 4.0
VMEM_LIMIT = 48 << 20
N_PARTS = 4
STOPS = (0, 1, 4, 8)


def lab_index(y, h, c):
    return (y * N_H + h) * N_CORE + c


PLACES = [(y, h, c) for y in range(N_Y) for h in range(N_H) for c in range(N_CORE)]
ACROSS = [(lab_index(y, h, c), lab_index(y, 1 - h, c)) for y, h, c in PLACES]
CORE = [(lab_index(y, h, c), lab_index(y, h, 1 - c)) for y, h, c in PLACES]
RINGS = [[lab_index(y, h, c) for y in range(N_Y)] for h in range(N_H) for c in range(N_CORE)]


def add_rows(core, d_ref, w_ref, rows_ref, before_ref, out_ref, arrive):
    pair = N_H * TILE
    for y in range(N_Y):
        if y in STOPS:
            arrive(STOPS.index(y)).wait()
        rows = rows_ref[y * pair:(y + 1) * pair, :]
        margins = lax.dot_general(
            d_ref[...], rows, (((1,), (1,)), ((), ())), preferred_element_type=jnp.float32
        )
        weights = jnp.concatenate([w_ref[lab_index(y, h, core)] for h in range(N_H)], axis=1)
        scaled = (weights.astype(jnp.float32) * margins).astype(jnp.bfloat16)
        part = jnp.dot(scaled, rows, preferred_element_type=jnp.float32)
        if y:
            out_ref[...] += part
        elif before_ref is None:
            out_ref[...] = part
        else:
            out_ref[...] = before_ref[...] + part


def fetch_rows(rows_hbm, rows_ref, rows_in, part):
    pair = N_H * TILE
    rows = pl.ds(STOPS[part] * pair, (STOPS[part + 1] - STOPS[part]) * pair)
    return pltpu.make_async_copy(rows_hbm.at[rows, :], rows_ref.at[rows, :], rows_in.at[part])


def own_kernel(
    core_ref, shortlist_ref, d_ref, active_hbm, rows_hbm, w_ref, out_ref, active_ref, rows_ref, active_in, rows_in
):
    tiles, labels = active_ref.shape[0] // TILE, active_ref.shape[1]
    per = tiles // N_PARTS

    def fetch_active(part):
        rows = pl.ds(part * per * TILE, per * TILE)
        return pltpu.make_async_copy(active_hbm.at[rows, :], active_ref.at[rows, :], active_in.at[part])

    def arrive(part):
        return fetch_rows(rows_hbm, rows_ref, rows_in, part)

    for part in range(N_PARTS):
        fetch_active(part).start()
    for part in range(len(STOPS) - 1):
        arrive(part).start()
    for t in range(tiles):
        if t % per == 0:
            fetch_active(t // per).wait()
        for j in range(labels // TILE):
            block = active_ref[t * TILE:(t + 1) * TILE, j * TILE:(j + 1) * TILE]
            block = (block * shortlist_ref[j, t]).astype(jnp.float32) * (1.0 / ROW_SCALE)
            w_ref[t, j * TILE:(j + 1) * TILE, :] = block.T.astype(jnp.bfloat16)
    add_rows(core_ref[0], d_ref, w_ref, rows_ref, None, out_ref, arrive)


def other_kernel(core_ref, d_ref, w_ref, rows_hbm, before_ref, out_ref, rows_ref, rows_in):
    def arrive(part):
        return fetch_rows(rows_hbm, rows_ref, rows_in, part)

    for part in range(len(STOPS) - 1):
        arrive(part).start()
    add_rows(core_ref[0], d_ref, w_ref, rows_ref, before_ref, out_ref, arrive)


SMEM, VMEM = pl.BlockSpec(memory_space=pltpu.SMEM), pl.BlockSpec(memory_space=pltpu.VMEM)
IN_PLACE = pl.BlockSpec(memory_space=pl.ANY)


def cost_of(slab, gathered):
    return pl.CostEstimate(
        flops=4 * slab.size * gathered.shape[0], bytes_accessed=2 * slab.size, transcendentals=0
    )


def own_sums(core, shortlist, gathered, active, slab):
    rows, labels = active.shape
    return pl.pallas_call(
        own_kernel,
        in_specs=[SMEM, SMEM, VMEM, IN_PLACE, IN_PLACE],
        out_specs=[VMEM, VMEM],
        out_shape=[
            jax.ShapeDtypeStruct((rows // TILE, labels, TILE), jnp.bfloat16),
            jax.ShapeDtypeStruct(gathered.shape, jnp.float32),
        ],
        scratch_shapes=[
            pltpu.VMEM(active.shape, jnp.int32),
            pltpu.VMEM(slab.shape, jnp.bfloat16),
            pltpu.SemaphoreType.DMA((N_PARTS,)),
            pltpu.SemaphoreType.DMA((len(STOPS) - 1,)),
        ],
        cost_estimate=cost_of(slab, gathered),
        compiler_params=pltpu.CompilerParams(vmem_limit_bytes=VMEM_LIMIT),
        name="own_sums",
    )(core, shortlist, gathered, active, slab)


def add_other(core, gathered, weights, slab, before):
    return pl.pallas_call(
        other_kernel,
        in_specs=[SMEM, VMEM, VMEM, IN_PLACE, VMEM],
        out_specs=VMEM,
        out_shape=jax.ShapeDtypeStruct(gathered.shape, jnp.float32),
        scratch_shapes=[
            pltpu.VMEM(slab.shape, jnp.bfloat16), pltpu.SemaphoreType.DMA((len(STOPS) - 1,)),
        ],
        input_output_aliases={4: 0},
        cost_estimate=cost_of(slab, gathered),
        compiler_params=pltpu.CompilerParams(vmem_limit_bytes=VMEM_LIMIT),
        name="add_other",
    )(core, gathered, weights, slab, before)


def repeat_kernel(in_ref, out_ref):
    for place in range(out_ref.shape[0]):
        out_ref[place] = in_ref[...]


def repeat(vectors, times):
    vmem = pl.BlockSpec(memory_space=pltpu.VMEM)
    return pl.pallas_call(
        repeat_kernel,
        in_specs=[vmem],
        out_specs=vmem,
        out_shape=jax.ShapeDtypeStruct((times, *vectors.shape), vectors.dtype),
        compiler_params=pltpu.CompilerParams(vmem_limit_bytes=4 << 20),
        name="repeat",
    )(vectors)


def label_scale(vectors):
    return jnp.maximum(jnp.max(jnp.abs(vectors.astype(jnp.float32)), axis=-1, keepdims=True), 1e-30)


def shards(features, direction, active, shortlist):
    return steps(features, direction[0], active, shortlist)


def steps(features, vectors, active, shortlist):
    lab = lax.axis_index("lab")
    h, core = (lab & N_CORE) // N_CORE, (lab & 1).astype(jnp.int32).reshape(1)
    across = lax.ppermute(features, "lab", ACROSS)
    gathered = lax.all_to_all(repeat(vectors, 16), "blk", 0, 0, tiled=True).reshape(-1, D)
    pair = jnp.where(h == 0, jnp.stack([features, across]), jnp.stack([across, features]))
    pair = (pair.astype(jnp.float32) * ROW_SCALE).astype(jnp.float16).reshape(-1, D)
    slab = lax.all_gather(pair, "lab", axis_index_groups=RINGS, axis=0, tiled=True)
    slab = slab.astype(jnp.bfloat16)
    beside = lax.ppermute(slab, "lab", CORE)
    weights, sums = own_sums(core, shortlist.T, gathered, active, slab)
    sums = add_other(1 - core, gathered, weights, beside, sums)
    sent = (sums * (1.0 / (SUM_SCALE * ROW_SCALE * label_scale(gathered)))).astype(jnp.float16)
    sent, own_scale = lax.optimization_barrier((sent, SUM_SCALE * label_scale(vectors)))
    pieces = lax.all_to_all(sent.reshape(16, 16, D), "blk", 0, 0, tiled=True)
    own_total = jnp.sum(pieces.astype(jnp.float32), axis=0) * own_scale
    product = vectors.astype(jnp.float32) + own_total
    curve = jnp.sum(vectors.astype(jnp.float32) * product, axis=-1) / D
    return (product[None], curve[None])


def solution(mesh):
    return jax.shard_map(
        shards,
        mesh=mesh,
        in_specs=(P(("blk", "lab"), None), P("lab", "blk", None), P("blk", "lab"), P("blk", "lab")),
        out_specs=(P("lab", "blk", None), P("lab", "blk")),
        check_vma=False,
    )
```

time: 109 us -> 111 us (1.018)
  waiting for transfers between devices: 15.7 us -> 18.7 us
    all_to_all x1, waiting for transfers between devices: 10.5 us -> 13.5 us  [steps(): lax.all_to_all(repeat(vectors, 16), 'blk', 0, 0, tiled=True).reshape(-1, D)]
    pallas_call x3 -> x2, Pallas kernels: 11 us -> 10.1 us  [the longest x1 6.26 us: own_sums(): pl.pallas_call(own_kernel, in_specs=[SMEM, SMEM, VMEM, IN_PLACE, IN_PLACE...]
  transfers between devices with their start and end apart: 3 -> 3, of which waited for: 2 -> 2; matrix products, arithmetic and copies ran while one was open for 0% -> 0% of each run, Pallas kernels for 7% -> 6%
where the time goes in v3:
time: 111 us
  blocking collectives  52 us (47%)
  starting transfers between devices  23.2 us (21%)
  waiting for transfers between devices  18.7 us (17%)
  Pallas kernels  10.9 us (10%)
  other arithmetic  5.16 us (5%)
    all_gather x1, blocking collectives, steps(): lax.all_gather(pair, 'lab', axis_index_groups=RINGS, axis=0, tiled=True)  35.5 us
    all_to_all x1, blocking collectives, steps(): pieces = lax.all_to_all(sent.reshape(16, 16, D), 'blk', 0, 0, tiled=True)  16.5 us
    all_to_all x1, waiting for transfers between devices, steps(): lax.all_to_all(repeat(vectors, 16), 'blk', 0, 0, tiled=True).reshape(-1, D)  13.5 us
    ppermute x1, starting transfers between devices, steps(): across = lax.ppermute(features, 'lab', ACROSS)  10.9 us
    all_to_all x1, starting transfers between devices, steps(): lax.all_to_all(repeat(vectors, 16), 'blk', 0, 0, tiled=True).reshape(-1, D)  10.4 us
    pallas_call x1, Pallas kernels, own_sums(): pl.pallas_call(own_kernel, in_specs=[SMEM, SMEM, VMEM, IN_PLACE, IN_PLACE...  6.26 us
    ppermute x1, waiting for transfers between devices, steps(): across = lax.ppermute(features, 'lab', ACROSS)  5.18 us
    pallas_call x1, Pallas kernels, add_other(): pl.pallas_call(other_kernel, in_specs=[SMEM, VMEM, VMEM, IN_PLACE, VMEM],...  3.81 us
  transfers between devices with their start and end apart: 3, of which 2 were waited for; matrix products, arithmetic and copies ran while one was open for 0% of the time, Pallas kernels for 6%

profile of v3, /device:TPU:24, one launch (start us, length us, event | category | flops | bytes accessed | tf_op | source)
XLA Modules:
  0.0 110.8 jit_solution(16405598689283928436)
XLA Ops:
  0.6 10.9 %collective-permute-start = (bf16[128,768]{1,0:T(8,128)(2,1)}, bf16[128,768]{1,0:T(8,128)(2,1)S(1)}, u32[]{:S(2)}, u32[]{:S(2)}) collective-permute-start(bf16[128,768]{1,0:T(8,128)(2,1)} %param.4), channel_id=1, source_target_pairs={{0,2},{1,3},{2,0},{3,1},{4,6},{5,7},{6,4},{7,5},{8,10},{9,11},{10,... | collective-permute-start | bytes 589832 | tf_op jit(solution)/shard_map/ppermute | solution.py:167
  11.6 5.2 %collective-permute-done = bf16[128,768]{1,0:T(8,128)(2,1)S(1)} collective-permute-done((bf16[128,768]{1,0:T(8,128)(2,1)}, bf16[128,768]{1,0:T(8,128)(2,1)S(1)}, u32[]{:S(2)}, u32[]{:S(2)}) %collective-permute-start) | collective-permute-done | bytes 196640 | tf_op jit(solution)/shard_map/ppermute | solution.py:167
  16.7 1.2 %multiply_convert_fusion.1 = f16[2,128,768]{2,1,0:T(8,128)(2,1)S(1)} fusion(bf16[1,128,768]{2,1,0:T(8,128)(2,1)S(1)} %bitcast.26, bf16[1,128,768]{2,1,0:T(8,128)(2,1)} %bitcast.25, pred[]{:T(512)S(6)} %eq.3), kind=kLoop, calls=%fused_computation.3 | loop fusion | flops 1179648 | bytes 786433 | tf_op jit(solution)/shard_map/convert_element_type | solution.py:170
  17.9 35.5 %all-gather.1 = f16[2048,768]{1,0:T(8,128)(2,1)S(1)} all-gather(f16[256,768]{1,0:T(8,128)(2,1)S(1)} %bitcast.23), channel_id=1, replica_groups={{0,4,8,12,16,20,24,28},{1,5,9,13,17,21,25,29},{2,6,10,14,18,22,26,30},{..., dimensions={0}, use_global_device_ids=true | all-gather | bytes 3538944 | tf_op jit(solution)/shard_map/all_gather | solution.py:171
  53.5 0.0 copy-start
  53.5 0.0 copy-start.1
  53.5 2.1 %convert_element_type.37.rows_hbm = bf16[2048,768]{1,0:T(8,128)(2,1)} convert(f16[2048,768]{1,0:T(8,128)(2,1)S(1)} %all-gather.1) | non-fusion elementwise | flops 1572864 | bytes 6291456 | tf_op jit(solution)/shard_map/convert_element_type | solution.py:172
  55.6 1.9 %collective-permute-start.1 = (bf16[2048,768]{1,0:T(8,128)(2,1)}, bf16[2048,768]{1,0:T(8,128)(2,1)}, u32[]{:S(2)}, u32[]{:S(2)}) collective-permute-start(bf16[2048,768]{1,0:T(8,128)(2,1)} %convert_element_type.37.rows_hbm), channel_id=1, source_target_pairs={{0,1},{1,0},{2,3},{3,2},{4,5},{5,4},{6,7},{7,6},{8,9},{9,8},{10,11... | collective-permute-start | bytes 9437192 | tf_op jit(solution)/shard_map/ppermute | solution.py:173
  57.5 0.0 copy-done
  57.5 0.8 repeat.1
  58.3 10.4 %all-to-all-start = ((bf16[16,16,768]{2,1,0:T(8,128)(2,1)}), bf16[16,16,768]{2,1,0:T(8,128)(2,1)S(1)}, u32[]{:S(2)}, u32[]{:S(2)}) async-start(bf16[16,16,768]{2,1,0:T(8,128)(2,1)} %repeat.1), calls=%async_computation | async-start | bytes 786432 | tf_op jit(solution)/shard_map/all_to_all | solution.py:168
  68.8 0.1 fusion
  68.9 13.5 %all-to-all-done = bf16[16,16,768]{2,1,0:T(8,128)(2,1)S(1)} async-done(((bf16[16,16,768]{2,1,0:T(8,128)(2,1)}), bf16[16,16,768]{2,1,0:T(8,128)(2,1)S(1)}, u32[]{:S(2)}, u32[]{:S(2)}) %all-to-all-start) | async-done | bytes 393248 | tf_op jit(solution)/shard_map/all_to_all | solution.py:168
  82.4 0.1 abs_reduce_fusion
  82.6 0.1 div.32
  82.7 0.0 copy-done.1
  82.7 6.3 %own_sums.1 = (bf16[32,256,128]{2,1,0:T(8,128)(2,1)S(1)}, f32[256,768]{1,0:T(8,128)S(1)}) custom-call(s32[1]{0:T(128)} %bitcast.core_ref, s32[2,32]{1,0:T(2,128)S(1)} %bitcast.22, bf16[256,768]{1,0:T(8,128)(2,1)S(1)} %bitcast.19, s32[4096,256]{1,0:T(8,128)} %active_hbm.1, bf16[2048,768]{1,0:T(8,128)(2,1)} %convert_element_type.37.rows_hbm), custom_call_target="tpu_custom_call" | custom-call | flops 1610612736 | bytes 3145728 | tf_op jit(solution)/shard_map/own_sums/pallas_call | solution.py:103
  88.9 0.0 collective-permute-done.1.rows_hbm
  88.9 3.8 %add_other.1 = f32[256,768]{1,0:T(8,128)S(1)} custom-call(s32[1]{0:T(128)S(6)} %sub.7.core_ref, bf16[256,768]{1,0:T(8,128)(2,1)S(1)} %bitcast.20, bf16[32,256,128]{2,1,0:T(8,128)(2,1)S(1)} %get-tuple-element.6.w_ref, bf16[2048,768]{1,0:T(8,128)(2,1)} %collective-permute-done.1.rows_hbm, ...), custom_call_target="tpu_custom_call", output_to_operand_aliasing={{}: (4, {})} | custom-call | flops 1610612736 | bytes 3145728 | tf_op jit(solution)/shard_map/add_other/pallas_call | solution.py:124
  92.8 0.1 multiply_convert_fusion
  92.9 16.5 %all_to_all.10 = f16[16,16,768]{2,1,0:T(8,128)(2,1)S(1)} all-to-all(f16[16,16,768]{2,1,0:T(8,128)(2,1)S(1)} %bitcast.24), channel_id=1, replica_groups=mesh['blk'=16,'lab'=32] {'blk'}, dimensions={0} | all-to-all | bytes 786432 | tf_op jit(solution)/shard_map/all_to_all | solution.py:178
  109.4 0.1 convert_reduce_fusion
  109.4 0.2 fusion.1
  109.6 0.7 fusion.2
  110.3 0.5 multiply_bitcast_fusion
  (2 shorter events, 0.0 us)
Async XLA Ops:
  0.6 16.1 %collective-permute-start = (bf16[128,768]{1,0:T(8,128)(2,1)}, bf16[128,768]{1,0:T(8,128)(2,1)S(1)}, u32[]{:S(2)}, u32[]{:S(2)}) collective-permute-start(bf16[128,768]{1,0:T(8,128)(2,1)} %param.4), channel_id=1, source_target_pairs={{0,2},{1,3},{2,0},{3,1},{4,6},{5,7},{6,4},{7,5},{8,10},{9,11},{10,... | collective-permute-start | bytes 589832 | tf_op jit(solution)/shard_map/ppermute | solution.py:167
  53.5 4.1 %copy-start = (bf16[1,16,768]{2,1,0:T(8,128)(2,1)S(1)}, bf16[1,16,768]{2,1,0:T(8,128)(2,1)}, u32[]{:S(2)}) copy-start(bf16[1,16,768]{2,1,0:T(8,128)(2,1)} %param.5) | copy-start | bytes 73732
  53.5 29.2 %copy-start.1 = (s32[32,2]{0,1:T(2,128)S(1)}, s32[32,2]{0,1:T(2,128)}, u32[]{:S(2)}) copy-start(s32[32,2]{0,1:T(2,128)} %param.7) | copy-start | bytes 772
  55.6 33.3 %collective-permute-start.1 = (bf16[2048,768]{1,0:T(8,128)(2,1)}, bf16[2048,768]{1,0:T(8,128)(2,1)}, u32[]{:S(2)}, u32[]{:S(2)}) collective-permute-start(bf16[2048,768]{1,0:T(8,128)(2,1)} %convert_element_type.37.rows_hbm), channel_id=1, source_target_pairs={{0,1},{1,0},{2,3},{3,2},{4,5},{5,4},{6,7},{7,6},{8,9},{9,8},{10,11... | collective-permute-start | bytes 9437192 | tf_op jit(solution)/shard_map/ppermute | solution.py:173
  58.3 24.1 %all-to-all-start = ((bf16[16,16,768]{2,1,0:T(8,128)(2,1)}), bf16[16,16,768]{2,1,0:T(8,128)(2,1)S(1)}, u32[]{:S(2)}, u32[]{:S(2)}) async-start(bf16[16,16,768]{2,1,0:T(8,128)(2,1)} %repeat.1), calls=%async_computation | async-start | bytes 786432 | tf_op jit(solution)/shard_map/all_to_all | solution.py:168
